TPU v7x, 32 devices: a whole 2x2x4 slice. The times are simulated.
32 devices in a mesh: cuts: 2 (over y), idx: 8 (over z, x), half: 2 (over core).
Axes of the slice: x: 2, y: 2, z: 4, core: 2. Of those that a mesh axis runs over, the one named last changes fastest.
Arguments:
- left_factor: float32 [2, 4, 64, 1024, 256], P('half', 'cuts', 'idx'), parts along dimension 1, may hold values from -6 to 6
- right_factor: float32 [2, 4, 64, 256, 1024], P('half', 'cuts', None, 'idx'), parts along dimension 1, may hold values from -0.25 to 0.25
Outputs:
- amplitudes: float32 [1024, 4, 1024], P(('idx', 'half'), 'cuts'), parts along dimension 1
There are 2 independent parts, one for each index of `cuts`. A program takes and returns all parts, laid end to end along the dimension named above; each array names one. Nothing has to cross between parts.
All inputs are finite; a program needn't handle non-finite values.
Results may differ from a plain program's by a relative error of at most 0.0003.
Values sent between devices are 32-bit elements; how exact they have to be, the bound alone decides.
A program may use at most 256 MiB of HBM per device.

v0:
```python
import math

import jax
import jax.numpy as jnp
from jax import lax
from jax.sharding import PartitionSpec as P

BATCH = 64
N = 1024


def swapped(x, axis, bit):
    return lax.ppermute(x, axis, [(i, i ^ 1 << bit) for i in range(lax.axis_size(axis))])


def complex_product(left_real, left_imag, right_real, right_imag, pattern):
    highest = lax.Precision.HIGHEST
    first_term = jnp.einsum(pattern, left_real, right_real, precision=highest)
    second_term = jnp.einsum(pattern, left_imag, right_imag, precision=highest)
    mixed_term = jnp.einsum(
        pattern, left_real + left_imag, right_real + right_imag, precision=highest
    )
    return (first_term - second_term, mixed_term - first_term - second_term)


def on_device(left_factor, right_factor):
    left_local = left_factor[0]
    right_local = right_factor[0]
    columns = lax.all_to_all(right_local, "idx", split_axis=1, concat_axis=2, tiled=True)
    real_part, imag_part = complex_product(
        left_local[0], left_local[1], columns[0], columns[1], "bmk,bkn->bmn"
    )
    merged = jnp.stack([real_part, imag_part])
    half_cols = merged.shape[3] // 2
    half_index = lax.axis_index("half")
    outgoing = lax.dynamic_slice_in_dim(merged, (1 - half_index) * half_cols, half_cols, 3)
    own_slab = lax.dynamic_slice_in_dim(merged, half_index * half_cols, half_cols, 3)
    other_slab = swapped(outgoing, "half", 0)
    is_lower = half_index == 0
    first_pair = jnp.where(is_lower, own_slab, other_slab)
    second_pair = jnp.where(is_lower, other_slab, own_slab)
    norm_scale = 1.0 / math.sqrt(2.0 * BATCH * N)
    real_part, imag_part = complex_product(
        first_pair[0], first_pair[1], second_pair[0], second_pair[1], "bmn,bon->mo"
    )
    return lax.psum_scatter(
        jnp.stack([real_part, imag_part], axis=1) * norm_scale,
        ("idx", "half"),
        scatter_dimension=0,
        tiled=True,
    )


def solution(mesh):
    return jax.shard_map(
        on_device,
        mesh=mesh,
        in_specs=(P("half", "cuts", "idx", None, None), P("half", "cuts", None, "idx", None)),
        out_specs=P(("idx", "half"), "cuts", None),
        check_vma=False,
    )
```

profile of v0, /device:TPU:0, one launch (start us, length us, event | category | flops | bytes accessed | tf_op | source)
XLA Modules:
  0.0 989.9 jit_solution(9931853911004770356)
XLA Ops:
  6.5 11.8 %copy.11 = f32[1,2,64,32,1024]{4,3,1,2,0:T(8,128)} copy(f32[1,2,64,32,1024]{4,3,2,1,0:T(8,128)} %param.3) | data formatting | bytes 33554432 | tf_op args[1]
  18.3 7.3 all-to-all-start
  25.6 0.0 reduce-scatter.2.cloned.1.call-start
  25.7 363.0 %all-to-all-done = f32[2,64,32,1024]{3,2,0,1:T(8,128)} async-done(((f32[2,64,32,1024]{3,2,0,1:T(8,128)}), f32[2,64,32,1024]{3,2,0,1:T(8,128)}, u32[]{:S(2)}, u32[]{:S(2)}) %all-to-all-start) | async-done | bytes 16777248 | tf_op jit(solution)/shard_map/all_to_all | solution.py:29
  388.7 11.8 %copy.10 = f32[2,8,8,32,1024]{4,3,1,2,0:T(8,128)} copy(f32[2,8,8,32,1024]{4,3,0,2,1:T(8,128)} %bitcast.2) | data formatting | bytes 33554432 | tf_op jit(solution)/shard_map/all_to_all | solution.py:29
  400.5 6.7 fusion.38
  407.2 0.0 copy-start.1
  407.2 0.0 copy-start
  407.3 34.2 %fusion.24 = f32[8,1024,1024]{2,1,0:T(8,128)} fusion(f32[8,256,1024]{2,1,0:T(8,128)S(1)} %bitcast.103, f32[1,2,8,1024,256]{4,3,2,1,0:T(8,128)} %param.2), kind=kOutput, calls=%fused_computation.36 | convolution fusion | flops 25769803776 | bytes 50331648 | tf_op jit(solution)/shard_map/bmk,bkn->bmn/dot_general | solution.py:18
  441.5 0.0 copy-done.1
  441.5 0.0 copy-done
  441.5 32.8 %fusion.21 = f32[8,1024,1024]{2,1,0:T(8,128)} fusion(f32[8,256,1024]{2,1,0:T(8,128)S(1)} %bitcast.101, f32[1,2,8,1024,256]{4,3,2,1,0:T(8,128)} %param.2), kind=kOutput, calls=%fused_computation.33 | convolution fusion | flops 25769803776 | bytes 50331648 | tf_op jit(solution)/shard_map/bmk,bkn->bmn/dot_general | solution.py:19
  474.3 55.7 %subtract_bitcast_fusion = f32[1,8,1024,1024]{3,2,1,0:T(8,128)} fusion(f32[8,1024,1024]{2,1,0:T(8,128)} %fusion.21, f32[8,1024,1024]{2,1,0:T(8,128)} %fusion.24, f32[8,256,1024]{2,1,0:T(8,128)} %bitcast.104, f32[8,256,1024]{2,1,0:T(8,128)} %bitcast.102, f32[1,2,8,1024,256]{4,3,2,1,0:T(8,128)} %param.2), kind=kOutput, calls=%fused_computation.6 | convolution fusion | flops 25790775296 | bytes 134217728 | tf_op jit(solution)/shard_map/bmk,bkn->bmn/dot_general | solution.py:20
  530.0 33.0 %subtract_bitcast_fusion.1 = f32[1,8,1024,1024]{3,2,1,0:T(8,128)} fusion(f32[8,1024,1024]{2,1,0:T(8,128)} %fusion.24, f32[8,1024,1024]{2,1,0:T(8,128)} %fusion.21), kind=kLoop, calls=%fused_computation.7 | loop fusion | flops 8388608 | bytes 100663296 | tf_op jit(solution)/shard_map/stack | solution.py:33
  563.0 23.0 %fusion = f32[2,8,1024,512]{3,2,1,0:T(8,128)} fusion(s32[]{:T(128)S(6)} %select_n.20, f32[1,8,1024,1024]{3,2,1,0:T(8,128)} %subtract_bitcast_fusion.1, f32[1,8,1024,1024]{3,2,1,0:T(8,128)} %subtract_bitcast_fusion), kind=kLoop, calls=%fused_computation.4 | loop fusion | flops 8388608 | bytes 100663296 | tf_op jit(solution)/shard_map/stack | solution.py:33
  586.0 0.0 collective-permute-start
  586.0 49.5 %collective-permute-done = f32[2,8,1024,512]{3,2,1,0:T(8,128)} collective-permute-done((f32[2,8,1024,512]{3,2,1,0:T(8,128)}, f32[2,8,1024,512]{3,2,1,0:T(8,128)}, u32[]{:S(2)}, u32[]{:S(2)}) %collective-permute-start) | collective-permute-done | bytes 33554464 | tf_op jit(solution)/shard_map/ppermute | solution.py:13
  635.5 54.2 %broadcast_select_fusion.1 = (f32[2,8,1024,512]{3,2,1,0:T(8,128)}, f32[2,8,1024,512]{3,2,1,0:T(8,128)}) fusion(f32[2,8,1024,512]{3,2,1,0:T(8,128)} %collective-permute-done, pred[]{:T(512)S(6)} %eq.3, s32[]{:T(128)S(6)} %select_n.19, f32[1,8,1024,1024]{3,2,1,0:T(8,128)} %subtract_bitcast_fusion, f32[1,8,1024,1024]{3,2,1,0:T(8,128)} %subtract_bitcast_fusion.1), kind=kLoop, calls=%fused_computation.22 | loop fusion | flops 33554432 | bytes 167772160 | tf_op jit(solution)/shard_map/jit(_where)/select_n | solution.py:40
  689.7 59.4 %fusion.5 = f32[1024,1024,1]{1,0,2:T(8,128)S(1)} fusion(f32[2,8,1024,512]{3,2,1,0:T(8,128)} %get-tuple-element.6, f32[2,8,1024,512]{3,2,1,0:T(8,128)} %get-tuple-element.5), kind=kOutput, calls=%fused_computation.11 | convolution fusion | flops 51539607552 | bytes 37748736 | tf_op jit(solution)/shard_map/bmn,bon->mo/dot_general | solution.py:19
  749.1 59.3 %fusion.8 = f32[1024,1024,1]{1,0,2:T(8,128)S(1)} fusion(f32[2,8,1024,512]{3,2,1,0:T(8,128)} %get-tuple-element.6, f32[2,8,1024,512]{3,2,1,0:T(8,128)} %get-tuple-element.5), kind=kOutput, calls=%fused_computation.14 | convolution fusion | flops 51539607552 | bytes 37748736 | tf_op jit(solution)/shard_map/bmn,bon->mo/dot_general | solution.py:18
  808.4 63.7 %fusion.32 = f32[1024,1,1024]{2,0,1:T(8,128)S(1)} fusion(f32[1024,1024,1]{1,0,2:T(8,128)S(1)} %fusion.5, f32[1024,1024,1]{1,0,2:T(8,128)S(1)} %fusion.8, f32[2,8,1024,512]{3,2,1,0:T(8,128)} %get-tuple-element.6, f32[2,8,1024,512]{3,2,1,0:T(8,128)} %get-tuple-element.5), kind=kOutput, calls=%fused_computation.45 | convolution fusion | flops 51550093312 | bytes 79691776 | tf_op jit(solution)/shard_map/bmn,bon->mo/dot_general | solution.py:20
  872.1 1.4 fusion.33
  873.5 4.3 maximum_multiply_fusion
  877.7 0.0 reduce-scatter.2.cloned.1.call-update
  877.8 102.6 %reduce-scatter.2.cloned.1.call-done = f32[64,2,1024]{2,0,1:T(8,128)} async-done(((f32[1024,2,1024]{2,0,1:T(8,128)}), f32[64,2,1024]{2,0,1:T(8,128)}) %reduce-scatter.2.cloned.1.call-update) | async-done | bytes 524304 | tf_op jit(solution)/shard_map/reduce_scatter | solution.py:46
  980.4 2.2 copy.7
Async XLA Ops:
  18.3 370.3 %all-to-all-start = ((f32[2,64,32,1024]{3,2,0,1:T(8,128)}), f32[2,64,32,1024]{3,2,0,1:T(8,128)}, u32[]{:S(2)}, u32[]{:S(2)}) async-start(f32[2,64,32,1024]{3,2,0,1:T(8,128)} %bitcast.105), calls=%async_computation | async-start | bytes 33554432 | tf_op jit(solution)/shard_map/all_to_all | solution.py:29
  25.6 954.7 %reduce-scatter.2.cloned.1.call-start = ((), (), s32[]{:S(2)}) async-start(), calls=%async_computation.2 | async-start | bytes 8912896 | tf_op jit(solution)/shard_map/reduce_scatter | solution.py:46
  407.2 34.3 %copy-start.1 = (f32[1,8,8,32,1024]{4,3,2,1,0:T(8,128)}, f32[1,8,8,32,1024]{4,3,2,1,0:T(8,128)S(1)}, u32[]{:S(2)}) copy-start(f32[1,8,8,32,1024]{4,3,2,1,0:T(8,128)S(1)} %get-tuple-element.8) | copy-start | bytes 25165828
  407.2 34.3 %copy-start = (f32[1,8,8,32,1024]{4,3,2,1,0:T(8,128)}, f32[1,8,8,32,1024]{4,3,2,1,0:T(8,128)S(1)}, u32[]{:S(2)}) copy-start(f32[1,8,8,32,1024]{4,3,2,1,0:T(8,128)S(1)} %get-tuple-element.7) | copy-start | bytes 25165828
  586.0 49.5 %collective-permute-start = (f32[2,8,1024,512]{3,2,1,0:T(8,128)}, f32[2,8,1024,512]{3,2,1,0:T(8,128)}, u32[]{:S(2)}, u32[]{:S(2)}) collective-permute-start(f32[2,8,1024,512]{3,2,1,0:T(8,128)} %fusion), channel_id=1, source_target_pairs={{0,1},{1,0},{2,3},{3,2},{4,5},{5,4},{6,7},{7,6},{8,9},{9,8},{10,11... | collective-permute-start | bytes 100663304 | tf_op jit(solution)/shard_map/ppermute | solution.py:13
Sparse Core Ops, SparseCore 0:
  877.9 102.4 reduce-scatter.1
where the time goes:
time: 997 us; the launch traced here: 990 us
  waiting for transfers between devices  515 us (52%)
  matrix products  305 us (31%)
  other arithmetic  116 us (12%)
  local copies, waits for them, and re-layouts  32.6 us (3%)
  between operations  13.9 us (1%)
    all_to_all x1, waiting for transfers between devices, on_device(): lax.all_to_all(right_local, 'idx', split_axis=1, concat_axis=2, tiled=True)  363 us
    dot_general x2, matrix products, complex_product(): jnp.einsum(pattern, left_real + left_imag, right_real + right_imag, preci...  119 us
    reduce_scatter x1, waiting for transfers between devices, on_device(): lax.psum_scatter(jnp.stack([real_part, imag_part], axis=1) * norm_scale,...  103 us
    dot_general x2, matrix products, complex_product(): first_term = jnp.einsum(pattern, left_real, right_real, precision=highest)  93.6 us
    dot_general x2, matrix products, complex_product(): second_term = jnp.einsum(pattern, left_imag, right_imag, precision=highest)  92.2 us
    another operation x2, other arithmetic, on_device(): merged = jnp.stack([real_part, imag_part])  56 us
    select_n x1, other arithmetic, on_device(): first_pair = jnp.where(is_lower, own_slab, other_slab)  54.2 us
    ppermute x1, waiting for transfers between devices, swapped(): lax.ppermute(x, axis, [(i, i ^ 1 << bit) for i in range(lax.axis_size(axi...  49.5 us
  transfers between devices with their start and end apart: 3, of which 3 were waited for; matrix products, arithmetic and copies ran while one was open for 0% of the time, Pallas kernels for 0%

commit v1 on v0

v1 whole, which is shorter than its diff:
```python
import math

import jax
import jax.numpy as jnp
from jax import lax
from jax.sharding import PartitionSpec as P

HIGH = lax.Precision.HIGH
CHUNKS = (3, 1)


def swapped(x, axis, bit):
    return lax.ppermute(x, axis, [(i, i ^ 1 << bit) for i in range(lax.axis_size(axis))])


def complex_product(left_real, left_imag, right_real, right_imag, pattern):
    first_term = jnp.einsum(pattern, left_real, right_real, precision=HIGH)
    second_term = jnp.einsum(pattern, left_imag, right_imag, precision=HIGH)
    mixed_term = jnp.einsum(
        pattern, left_real + left_imag, right_real + right_imag, precision=HIGH
    )
    return (first_term - second_term, mixed_term - first_term - second_term)


def by_columns(left_local, right_local, norm_scale):
    columns = lax.all_to_all(right_local, "idx", split_axis=1, concat_axis=2, tiled=True)
    merged = jnp.stack(
        complex_product(left_local[0], left_local[1], columns[0], columns[1], "bmk,bkn->bmn")
    )
    half_cols = merged.shape[3] // 2
    half_index = lax.axis_index("half")
    outgoing = lax.dynamic_slice_in_dim(merged, (1 - half_index) * half_cols, half_cols, 3)
    own_slab = lax.dynamic_slice_in_dim(merged, half_index * half_cols, half_cols, 3)
    other_slab = swapped(outgoing, "half", 0)
    is_lower = half_index == 0
    first_pair = jnp.where(is_lower, own_slab, other_slab)
    second_pair = jnp.where(is_lower, other_slab, own_slab)
    real_part, imag_part = complex_product(
        first_pair[0], first_pair[1], second_pair[0], second_pair[1], "bmn,bon->mo"
    )
    return jnp.stack([real_part, imag_part], axis=1) * norm_scale


def by_batch(left_local, right_local, norm_scale):
    idx, half = lax.axis_size("idx"), lax.axis_size("half")
    planes, batch, rows, between = right_local.shape
    mine = left_local.shape[1] // half
    half_index = lax.axis_index("half")
    blocks = right_local.reshape(planes, idx * half, mine, rows, between)
    sizes = CHUNKS if sum(CHUNKS) == mine else (mine,)
    received = []
    start = 0
    for size in sizes:
        piece = blocks[:, :, start:start + size].transpose(1, 0, 2, 3, 4)
        received.append(
            lax.all_to_all(piece, ("idx", "half"), split_axis=0, concat_axis=0, tiled=True)
        )
        start += size
    outgoing = lax.dynamic_slice_in_dim(left_local, (1 - half_index) * mine, mine, 1)
    own = lax.dynamic_slice_in_dim(left_local, half_index * mine, mine, 1)
    other = swapped(outgoing, "half", 0)
    is_lower = half_index == 0
    first = jnp.where(is_lower, own, other)
    second = jnp.where(is_lower, other, own)
    total = None
    start = 0
    for size, got in zip(sizes, received):
        got = got.reshape(idx, half, planes, size, rows, between)
        pairs = got.transpose(1, 2, 3, 0, 4, 5).reshape(half, planes, size, idx * rows, between)
        inner = complex_product(
            pairs[0, 0], pairs[0, 1], pairs[1, 0], pairs[1, 1], "bkn,bln->bkl"
        )
        a = first[:, start:start + size]
        b = second[:, start:start + size]
        partial = complex_product(a[0], a[1], inner[0], inner[1], "bmk,bkl->bml")
        term = complex_product(partial[0], partial[1], b[0], b[1], "bml,bol->mo")
        total = term if total is None else (total[0] + term[0], total[1] + term[1])
        start += size
    return jnp.stack(total, axis=1) * norm_scale


def on_device(left_factor, right_factor):
    left_local = left_factor[0]
    right_local = right_factor[0]
    batch, between = right_local.shape[1], right_local.shape[3]
    norm_scale = 1.0 / math.sqrt(2.0 * batch * between)
    shared = left_local.shape[1] % lax.axis_size("half") == 0
    form = by_batch if shared else by_columns
    return lax.psum_scatter(
        form(left_local, right_local, norm_scale),
        ("idx", "half"),
        scatter_dimension=0,
        tiled=True,
    )


def solution(mesh):
    return jax.shard_map(
        on_device,
        mesh=mesh,
        in_specs=(P("half", "cuts", "idx", None, None), P("half", "cuts", None, "idx", None)),
        out_specs=P(("idx", "half"), "cuts", None),
        check_vma=False,
    )
```

time: 997 us -> 584 us (0.59)
  matrix products: 305 us -> 62.5 us
  waiting for transfers between devices: 515 us -> 396 us
  other arithmetic: 116 us -> 24.1 us
  local copies, waits for them, and re-layouts: 32.6 us -> 53.6 us
  starting transfers between devices: 7.32 us -> 27.5 us
    dot_general x4 -> x12, matrix products: 186 us -> 38.8 us  [the longest x6 20.8 us: complex_product(): first_term = jnp.einsum(pattern, left_real, right_real, precision=HIGH)]
    all_to_all x1 -> x2, waiting for transfers between devices: 363 us -> 235 us  [by_batch(): lax.all_to_all(piece, ('idx', 'half'), split_axis=0, concat_axis=0, tiled...]
    dot_general x2 -> x6, matrix products: 119 us -> 23.6 us  [complex_product(): jnp.einsum(pattern, left_real + left_imag, right_real + right_imag, preci...]
    reduce_scatter x1, waiting for transfers between devices: 103 us -> 152 us  [on_device(): lax.psum_scatter(form(left_local, right_local, norm_scale), ('idx', 'half...]
    another operation x3 -> x1, other arithmetic: 57.4 us -> 8.7 us  [by_batch(): return jnp.stack(total, axis=1) * norm_scale]
    select_n x1, other arithmetic: 54.2 us -> 6.72 us  [by_batch(): second = jnp.where(is_lower, other, own)]
    transpose x0 -> x6, local copies, waits for them, and re-layouts: none -> 42.8 us  [the longest x4 28.4 us: by_batch(): piece = blocks[:, :, start:start + size].transpose(1, 0, 2, 3, 4)]
    ppermute x1, waiting for transfers between devices: 49.5 us -> 8.71 us  [swapped(): lax.ppermute(x, axis, [(i, i ^ 1 << bit) for i in range(lax.axis_size(axi...]
  transfers between devices with their start and end apart: 3 -> 4, of which waited for: 3 -> 4; matrix products, arithmetic and copies ran while one was open for 0% -> 10% of each run, Pallas kernels for 0% -> 0%
where the time goes in v1:
time: 584 us; the launch traced here: 578 us
  waiting for transfers between devices  396 us (68%)
  matrix products  62.5 us (11%)
  local copies, waits for them, and re-layouts  53.6 us (9%)
  starting transfers between devices  27.5 us (5%)
  other arithmetic  24.1 us (4%)
  between operations  14.1 us (2%)
    all_to_all x2, waiting for transfers between devices, by_batch(): lax.all_to_all(piece, ('idx', 'half'), split_axis=0, concat_axis=0, tiled...  235 us
    reduce_scatter x1, waiting for transfers between devices, on_device(): lax.psum_scatter(form(left_local, right_local, norm_scale), ('idx', 'half...  152 us
    transpose x4, local copies, waits for them, and re-layouts, by_batch(): piece = blocks[:, :, start:start + size].transpose(1, 0, 2, 3, 4)  28.4 us
    all_to_all x2, starting transfers between devices, by_batch(): lax.all_to_all(piece, ('idx', 'half'), split_axis=0, concat_axis=0, tiled...  27.1 us
    dot_general x6, matrix products, complex_product(): jnp.einsum(pattern, left_real + left_imag, right_real + right_imag, preci...  23.6 us
    dot_general x6, matrix products, complex_product(): first_term = jnp.einsum(pattern, left_real, right_real, precision=HIGH)  20.8 us
    dot_general x6, matrix products, complex_product(): second_term = jnp.einsum(pattern, left_imag, right_imag, precision=HIGH)  18 us
    transpose x2, local copies, waits for them, and re-layouts, by_batch(): got.transpose(1, 2, 3, 0, 4, 5)  14.3 us
  transfers between devices with their start and end apart: 4, of which 4 were waited for; matrix products, arithmetic and copies ran while one was open for 10% of the time, Pallas kernels for 0%

profile of v1, /device:TPU:0, one launch (start us, length us, event | category | flops | bytes accessed | tf_op | source)
XLA Modules:
  0.0 578.1 jit_solution(6922426632892912840)
XLA Ops:
  6.5 2.5 slice_bitcast_fusion.1
  9.0 2.3 copy.17
  11.3 7.4 %all-to-all-start.1 = ((f32[16,2,1,32,1024]{4,3,2,1,0:T(8,128)}), f32[16,2,1,32,1024]{4,3,2,1,0:T(8,128)}, u32[]{:S(2)}, u32[]{:S(2)}) async-start(f32[16,2,1,32,1024]{4,3,2,1,0:T(8,128)} %copy.17), calls=%async_computation.1 | async-start | bytes 8388608 | tf_op jit(solution)/shard_map/all_to_all | solution.py:56
  18.8 11.8 %slice_bitcast_fusion = f32[16,2,3,32,1024]{4,3,2,0,1:T(8,128)} fusion(f32[2,16,4,32,1024]{4,3,2,1,0:T(8,128)} %bitcast.163), kind=kLoop, calls=%fused_computation | loop fusion | bytes 25165824 | tf_op jit(solution)/shard_map/transpose | solution.py:54
  30.6 11.8 %copy.15 = f32[16,2,3,32,1024]{4,3,2,1,0:T(8,128)} copy(f32[16,2,3,32,1024]{4,3,2,0,1:T(8,128)} %slice_bitcast_fusion) | data formatting | bytes 25165824 | tf_op jit(solution)/shard_map/transpose | solution.py:54
  42.4 53.9 %all-to-all-done.1 = f32[16,2,1,32,1024]{4,3,2,1,0:T(8,128)} async-done(((f32[16,2,1,32,1024]{4,3,2,1,0:T(8,128)}), f32[16,2,1,32,1024]{4,3,2,1,0:T(8,128)}, u32[]{:S(2)}, u32[]{:S(2)}) %all-to-all-start.1) | async-done | bytes 4194336 | tf_op jit(solution)/shard_map/all_to_all | solution.py:56
  96.3 19.7 %all-to-all-start = ((f32[16,2,3,32,1024]{4,3,2,1,0:T(8,128)}), f32[16,2,3,32,1024]{4,3,2,1,0:T(8,128)}, u32[]{:S(2)}, u32[]{:S(2)}) async-start(f32[16,2,3,32,1024]{4,3,2,1,0:T(8,128)} %copy.15), calls=%async_computation | async-start | bytes 25165824 | tf_op jit(solution)/shard_map/all_to_all | solution.py:56
  116.0 0.0 reduce-scatter.2.cloned.1.call-start
  116.1 7.2 %dynamic-slice_bitcast_fusion = f32[2,4,1024,256]{3,2,1,0:T(8,128)} fusion(f32[1,2,8,1024,256]{4,3,2,1,0:T(8,128)} %param.2, s32[]{:T(128)S(6)} %select_n.20), kind=kLoop, calls=%fused_computation.4 | loop fusion | bytes 16777220 | tf_op jit(solution)/shard_map/dynamic_slice | solution.py:59
  123.2 0.4 collective-permute-start
  123.6 2.5 copy.18
  126.1 0.6 fusion.50
  126.7 0.6 fusion.53
  127.3 0.7 fusion.38
  128.0 8.7 %collective-permute-done = f32[2,4,1024,256]{3,2,1,0:T(8,128)} collective-permute-done((f32[2,4,1024,256]{3,2,1,0:T(8,128)}, f32[2,4,1024,256]{3,2,1,0:T(8,128)}, u32[]{:S(2)}, u32[]{:S(2)}) %collective-permute-start) | collective-permute-done | bytes 8388640 | tf_op jit(solution)/shard_map/ppermute | solution.py:13
  136.7 6.7 %bitcast_select_fusion = (f32[2,4,1024,256]{3,2,1,0:T(8,128)S(1)}, f32[2,4,1024,256]{3,2,1,0:T(8,128)S(1)}) fusion(f32[2,4,1024,256]{3,2,1,0:T(8,128)} %collective-permute-done, f32[1,2,8,1024,256]{4,3,2,1,0:T(8,128)} %param.2, s32[]{:T(128)S(6)} %select_n.19, pred[]{:T(512)S(6)} %eq.3), kind=kLoop, calls=%fused_computation.2 | loop fusion | flops 4194304 | bytes 33554436 | tf_op jit(solution)/shard_map/jit(_where)/select_n | solution.py:64
  143.5 0.0 copy-start.1
  143.5 0.0 copy-start.2
  143.5 0.6 fusion.48
  144.1 0.6 fusion.56
  144.7 0.6 fusion.23
  145.3 1.4 copy-done.1
  146.7 3.8 fusion.41
  150.5 3.9 fusion.44
  154.4 0.0 copy-done.2
  154.4 3.8 fusion.39
  158.2 181.4 %all-to-all-done = f32[16,2,3,32,1024]{4,3,2,1,0:T(8,128)} async-done(((f32[16,2,3,32,1024]{4,3,2,1,0:T(8,128)}), f32[16,2,3,32,1024]{4,3,2,1,0:T(8,128)}, u32[]{:S(2)}, u32[]{:S(2)}) %all-to-all-start) | async-done | bytes 12582944 | tf_op jit(solution)/shard_map/all_to_all | solution.py:56
  339.6 11.8 %copy.16 = f32[2,2,3,8,32,1024]{5,4,3,2,1,0:T(8,128)} copy(f32[2,2,3,8,32,1024]{5,4,2,1,0,3:T(8,128)} %bitcast.6) | data formatting | bytes 25165824 | tf_op jit(solution)/shard_map/transpose | solution.py:69
  351.5 4.6 fusion.15
  356.0 0.0 slice-start
  356.0 5.4 fusion.14
  361.4 0.0 copy-done
  361.5 0.0 slice-start.1
  361.5 1.8 fusion.33
  363.2 3.4 fusion.13
  366.7 0.0 slice-done
  366.7 0.0 slice-start.2
  366.7 1.5 fusion.16
  368.2 0.0 slice-start.3
  368.3 3.5 subtract_subtract_fusion
  371.8 6.9 %fusion.17 = f32[1024,1024,1]{1,0,2:T(8,128)} fusion(f32[2,4,1024,256]{3,2,1,0:T(8,128)S(1)} %bitcast.158, f32[3,1024,256]{2,1,0:T(8,128)S(1)} %fusion.13, f32[3,1024,256]{2,1,0:T(8,128)S(1)} %fusion.16), kind=kOutput, calls=%fused_computation.34 | convolution fusion | flops 4832624640 | bytes 13631488 | tf_op jit(solution)/shard_map/bml,bol->mo/dot_general | solution.py:17
  378.7 6.9 %fusion.18 = f32[1024,1024,1]{1,0,2:T(8,128)} fusion(f32[3,1024,256]{2,1,0:T(8,128)S(1)} %copy-done.4, f32[2,4,1024,256]{3,2,1,0:T(8,128)S(1)} %bitcast.158), kind=kOutput, calls=%fused_computation.35 | convolution fusion | flops 4831838208 | bytes 10485760 | tf_op jit(solution)/shard_map/bml,bol->mo/dot_general | solution.py:18
  385.6 8.7 %fusion.4 = f32[1024,1,1024]{2,0,1:T(8,128)} fusion(f32[1024,1024,1]{1,0,2:T(8,128)} %fusion.18, f32[1024,1024,1]{1,0,2:T(8,128)} %fusion.17, f32[1024,1024]{1,0:T(8,128)S(1)} %copy-done.3, f32[1024,1024]{1,0:T(8,128)} %fusion.41), kind=kLoop, calls=%fused_computation.12 | loop fusion | flops 3145728 | bytes 20971520 | tf_op jit(solution)/shard_map/stack | solution.py:79
  394.3 13.3 %fusion.2 = f32[1024,1,1024]{2,0,1:T(8,128)} fusion(f32[1024,1024,1]{1,0,2:T(8,128)} %fusion.18, f32[1024,1024,1]{1,0,2:T(8,128)} %fusion.17, f32[1024,1024]{1,0:T(8,128)} %fusion.41, f32[1024,1024]{1,0:T(8,128)} %fusion.39, f32[1024,1024]{1,0:T(8,128)S(1)} %copy-done.3, f32[2,4,1024,256]{3,2,1,0:T(8,128)} %copy-done.2, ...), kind=kOutput, calls=%fused_computation.9 | convolution fusion | flops 4839440384 | bytes 40894464 | tf_op jit(solution)/shard_map/bml,bol->mo/dot_general | solution.py:19
  407.6 8.7 %maximum_multiply_fusion = f32[1024,2,1024]{2,0,1:T(8,128)} fusion(f32[1024,1,1024]{2,0,1:T(8,128)} %fusion.2, f32[1024,1,1024]{2,0,1:T(8,128)} %fusion.4), kind=kLoop, calls=%fused_computation.1 | loop fusion | flops 4194304 | bytes 16777216 | tf_op jit(solution)/shard_map/mul | solution.py:79
  416.3 0.0 reduce-scatter.2.cloned.1.call-update
  416.3 152.3 %reduce-scatter.2.cloned.1.call-done = f32[64,2,1024]{2,0,1:T(8,128)} async-done(((f32[1024,2,1024]{2,0,1:T(8,128)}), f32[64,2,1024]{2,0,1:T(8,128)}) %reduce-scatter.2.cloned.1.call-update) | async-done | bytes 524304 | tf_op jit(solution)/shard_map/reduce_scatter | solution.py:89
  568.6 2.2 copy.19
  (10 shorter events, 0.0 us)
Async XLA Ops:
  11.3 85.0 %all-to-all-start.1 = ((f32[16,2,1,32,1024]{4,3,2,1,0:T(8,128)}), f32[16,2,1,32,1024]{4,3,2,1,0:T(8,128)}, u32[]{:S(2)}, u32[]{:S(2)}) async-start(f32[16,2,1,32,1024]{4,3,2,1,0:T(8,128)} %copy.17), calls=%async_computation.1 | async-start | bytes 8388608 | tf_op jit(solution)/shard_map/all_to_all | solution.py:56
  96.3 243.3 %all-to-all-start = ((f32[16,2,3,32,1024]{4,3,2,1,0:T(8,128)}), f32[16,2,3,32,1024]{4,3,2,1,0:T(8,128)}, u32[]{:S(2)}, u32[]{:S(2)}) async-start(f32[16,2,3,32,1024]{4,3,2,1,0:T(8,128)} %copy.15), calls=%async_computation | async-start | bytes 25165824 | tf_op jit(solution)/shard_map/all_to_all | solution.py:56
  116.0 452.6 %reduce-scatter.2.cloned.1.call-start = ((), (), s32[]{:S(2)}) async-start(), calls=%async_computation.3 | async-start | bytes 8912896 | tf_op jit(solution)/shard_map/reduce_scatter | solution.py:89
  123.2 13.5 %collective-permute-start = (f32[2,4,1024,256]{3,2,1,0:T(8,128)}, f32[2,4,1024,256]{3,2,1,0:T(8,128)}, u32[]{:S(2)}, u32[]{:S(2)}) collective-permute-start(f32[2,4,1024,256]{3,2,1,0:T(8,128)} %dynamic-slice_bitcast_fusion), channel_id=1, source_target_pairs={{0,1},{1,0},{2,3},{3,2},{4,5},{5,4},{6,7},{7,6},{8,9},{9,8},{10,11... | collective-permute-start | bytes 25165832 | tf_op jit(solution)/shard_map/ppermute | solution.py:13
  143.5 3.2 copy-start.1
  143.5 10.9 %copy-start.2 = (f32[2,4,1024,256]{3,2,1,0:T(8,128)}, f32[2,4,1024,256]{3,2,1,0:T(8,128)S(1)}, u32[]{:S(2)}) copy-start(f32[2,4,1024,256]{3,2,1,0:T(8,128)S(1)} %get-tuple-element.5) | copy-start | bytes 25165828
  351.5 10.0 %copy-start = (f32[2,2,3,8,32,1024]{5,4,3,2,1,0:T(8,128)S(1)}, f32[2,2,3,8,32,1024]{5,4,3,2,1,0:T(8,128)}, u32[]{:S(2)}) copy-start(f32[2,2,3,8,32,1024]{5,4,3,2,1,0:T(8,128)} %copy.16) | copy-start | bytes 37748740
  356.0 10.6 %slice-start = ((s8[8388608]{0:T(1024)(128)(4,1)}), s8[4194304]{0:T(1024)(128)(4,1)S(1)}, s32[]{:S(2)}) async-start(s8[8388608]{0:T(1024)(128)(4,1)} %bitcast.155), calls=%async_computation.4 | async-start | bytes 8388608
  361.5 5.2 slice-start.1
  366.7 5.1 slice-start.2
  368.2 3.5 slice-start.3
  371.8 6.9 %copy-start.4 = (f32[3,1024,256]{2,1,0:T(8,128)S(1)}, f32[3,1024,256]{2,1,0:T(8,128)}, u32[]{:S(2)}) copy-start(f32[3,1024,256]{2,1,0:T(8,128)} %subtract_subtract_fusion) | copy-start | bytes 9437188
  378.7 7.0 %copy-start.3 = (f32[1024,1024]{1,0:T(8,128)S(1)}, f32[1024,1024]{1,0:T(8,128)}, u32[]{:S(2)}) copy-start(f32[1024,1024]{1,0:T(8,128)} %fusion.44) | copy-start | bytes 12582916
Sparse Core Ops, SparseCore 0:
  416.4 152.1 reduce-scatter.1
